TPU v7x, 256 devices: a whole 4x4x8 slice. The times are simulated.
256 devices in a mesh: row: 32 (over z, y_lo, core), col: 8 (over x, y_hi).
Axes of the slice: x: 4, y: 4 (y_hi: 2, y_lo: 2; y = y_hi * 2 + y_lo), z: 8, core: 2. Of those that a mesh axis runs over, the one named last changes fastest.
Arguments:
- acts: bfloat16 [1024, 16384], P(None, 'col'), may hold values from -6 to 6
- grads: bfloat16 [1024, 16384], P(None, 'row'), may hold values from -0.1875 to 0.1875
- row_roots: bfloat16 [16384, 1024], P('row'), as said below
- col_stats: float32 [1024, 16384], P('row', 'col'), as said below
Outputs:
- update: bfloat16 [16384, 16384], P('row', 'col')
- new_stats: float32 [1024, 16384], P('row', 'col')
- new_roots: float32 [1024, 16384], P('row', 'col')
Inputs may be any that keep to these rules, and one draw needn't show every extreme that they name: `col_stats`: each block of 1024 columns is symmetric positive definite. `row_roots`: each block of 1024 rows is symmetric.
All inputs are finite; a program needn't handle non-finite values.
Results may differ from a plain program's by a relative error of at most 0.0015.
The roundings to bfloat16 on the way count: a program that leaves them out, or rounds other values in their place, can miss the bound.
Values may be sent and summed in bfloat16 or wider, within the bound.
No kernel may reach another device: no remote copies, remote signals or barrier semaphores. Data moves between devices by JAX's collectives and lax.ppermute only.
A program may use at most 128 MiB of HBM per device.

v0:
```python
import jax
import jax.numpy as jnp
from jax import lax
from jax.sharding import PartitionSpec as P

decay_rate = 0.75
damping = 0.001
epsilon = 1e-06


def partner(block, axis, bit):
    count = lax.axis_size(axis)
    route = []
    for low in range(count):
        high = low | 1 << bit
        if high != low and high < count:
            route += [(low, high), (high, low)]
    return lax.ppermute(block, axis, route)


def shards(acts, grads, row_roots, col_stats):
    contract_first = (((0,), (0,)), ((), ()))
    block_size = row_roots.shape[1]
    weight_rows = grads.shape[1]
    weight_cols = acts.shape[1]
    stat_rows = col_stats.shape[0]
    block_count = weight_cols // block_size
    total_rows = weight_rows * lax.axis_size("row")
    own_tile = lax.dot_general(
        grads, acts, contract_first, preferred_element_type=jnp.float32
    ).astype(jnp.bfloat16)
    other_tile = partner(own_tile, "row", 0)
    is_lower = lax.axis_index("row") % 2 == 0
    paired = jnp.where(
        is_lower,
        jnp.concatenate([own_tile, other_tile], 0),
        jnp.concatenate([other_tile, own_tile], 0),
    )
    whitened = jnp.dot(row_roots, paired, preferred_element_type=jnp.float32).astype(jnp.bfloat16)
    pieces = []
    for column_index_block in range(block_count):
        left = lax.dynamic_slice_in_dim(
            whitened, column_index_block * block_size, stat_rows * lax.axis_size("row"), 1
        )
        right = whitened[:, column_index_block * block_size : (column_index_block + 1) * block_size]
        pieces.append(
            lax.dot_general(left, right, contract_first, preferred_element_type=jnp.float32)
        )
    summed = lax.psum_scatter(jnp.concatenate(pieces, 1), "row", scatter_dimension=0, tiled=True)
    mix = (1.0 - decay_rate) / total_rows
    new_stats = decay_rate * col_stats + mix * summed
    full_stats = lax.all_gather(new_stats, "row", axis=0, tiled=True)
    first_row = lax.axis_index("row") * stat_rows
    identity = jnp.eye(block_size, dtype=jnp.float32)
    row_iota = lax.broadcasted_iota(jnp.int32, (stat_rows, block_size), 0) + first_row
    col_iota = lax.broadcasted_iota(jnp.int32, (stat_rows, block_size), 1)
    identity_rows = (row_iota == col_iota).astype(jnp.float32)
    scales = []
    starts = []
    factors = []
    for index_block in range(block_count):
        shifted = (
            full_stats[:, index_block * block_size : (index_block + 1) * block_size]
            + damping * identity
        )
        norm_scale = 2.0 * jnp.trace(shifted) / block_size
        start_iterate = shifted / norm_scale
        scales.append(norm_scale)
        starts.append(start_iterate)
        factors.append(1.5 * identity - 0.5 * start_iterate)
    seconds = [
        jnp.dot(starts[k], factors[k], precision=lax.Precision.HIGHEST) for k in range(block_count)
    ]
    root_pieces = []
    for index_block in range(block_count):
        factor_rows = lax.dynamic_slice_in_dim(factors[index_block], first_row, stat_rows, 0)
        product_rows = jnp.dot(factor_rows, seconds[index_block], precision=lax.Precision.HIGHEST)
        second_factor = 1.5 * identity_rows - 0.5 * product_rows
        root_rows = jnp.dot(second_factor, factors[index_block], precision=lax.Precision.HIGHEST)
        root_pieces.append(root_rows / jnp.sqrt(scales[index_block]))
    new_roots = jnp.concatenate(root_pieces, 1)
    roots_half = new_roots.astype(jnp.bfloat16)
    empty = jnp.zeros((weight_rows, weight_cols), jnp.float32)
    piece = lax.all_gather(roots_half, "row", axis=0, tiled=True)
    terms = []
    for index_block in range(block_count):
        left = lax.dynamic_slice_in_dim(whitened, index_block * block_size, piece.shape[0], 1)
        right = piece[:, index_block * block_size : (index_block + 1) * block_size]
        terms.append(jnp.dot(left, right, preferred_element_type=jnp.float32))
    product = empty + jnp.concatenate(terms, 1)
    grad_square = jnp.sum(jnp.square(own_tile.astype(jnp.float32)))
    prod_square = jnp.sum(jnp.square(product))
    grad_total, prod_total = lax.psum((grad_square, prod_square), ("row", "col"))
    update = (product * jnp.sqrt(grad_total / (prod_total + epsilon))).astype(jnp.bfloat16)
    return (update, new_stats, new_roots)


def solution(mesh):
    return jax.shard_map(
        shards,
        mesh=mesh,
        in_specs=(P(None, "col"), P(None, "row"), P("row", None), P("row", "col")),
        out_specs=(P("row", "col"), P("row", "col"), P("row", "col")),
        check_vma=False,
    )
```

profile of v0, /device:TPU:1, one launch (start us, length us, event | category | flops | bytes accessed | tf_op | source)
XLA Modules:
  0.0 459.7 jit_solution(10663552201860508157)
XLA Ops:
  8.4 5.7 %multiply_reduce_fusion.1 = (f32[]{:T(128)}, bf16[512,2048]{1,0:T(8,128)(2,1)S(1)}) fusion(bf16[1024,512]{1,0:T(8,128)(2,1)S(1)} %copy-done, bf16[1024,2048]{1,0:T(8,128)(2,1)} %param.4), kind=kOutput, calls=%fused_computation.15 | convolution fusion | flops 2151677952 | bytes 7340036 | tf_op jit(solution)/shard_map/dot_general | solution.py:29
  14.1 3.2 collective-permute-start
  17.4 3.9 collective-permute-done
  21.3 4.9 %fusion.10 = bf16[512,2048]{0,1:T(8,128)(2,1)S(1)} fusion(bf16[512,1024]{1,0:T(8,128)(2,1)} %param.6, bf16[512,2048]{1,0:T(8,128)(2,1)} %collective-permute-done, bf16[512,2048]{1,0:T(8,128)(2,1)S(1)} %get-tuple-element.18, pred[]{:T(512)S(6)} %eq.24), kind=kOutput, calls=%fused_computation.24 | convolution fusion | flops 2167406592 | bytes 7340033 | tf_op jit(solution)/shard_map/dot_general | solution.py:39
  27.5 1.3 fusion.21
  28.8 4.1 pad_maximum_fusion
  32.9 9.2 %copy.12 = f32[1024,2048]{1,0:T(8,128)} copy(f32[1024,2048]{0,1:T(8,128)} %pad_maximum_fusion) | data formatting | bytes 16777216
  43.4 126.7 %reduce-scatter.4.cloned.1.call-done = f32[32,2048]{1,0:T(8,128)} async-done(((f32[1024,2048]{1,0:T(8,128)}), f32[32,2048]{1,0:T(8,128)}) %reduce-scatter.4.cloned.1.call-update) | async-done | bytes 262160
  172.6 74.8 %all-gather.3.cloned.1.call-done = f32[1024,2048]{1,0:T(8,128)} async-done(((f32[32,2048]{1,0:T(8,128)}), f32[1024,2048]{1,0:T(8,128)}) %all-gather.3.cloned.1.call-update) | async-done | bytes 8388624 | tf_op jit(solution)/shard_map/all_gather | solution.py:52
  247.3 4.3 select_reduce_fusion.1
  253.1 5.1 %select_subtract_fusion.1 = (f32[1024,1024]{1,0:T(8,128)S(1)}, f32[1024,1024]{1,0:T(8,128)S(1)}) fusion(f32[]{:T(128)S(6)} %div.33, f32[1024,2048]{1,0:T(8,128)} %all-gather.3.cloned.1.call-done, f32[]{:T(128)S(6)} %div.38), kind=kLoop, calls=%fused_computation.4 | loop fusion | flops 11534336 | bytes 16777224 | tf_op jit(solution)/shard_map/sub | solution.py:70
  258.9 13.5 %fusion.25 = f32[1024,1024]{1,0:T(8,128)S(1)} fusion(f32[1024,1024]{1,0:T(8,128)S(1)} %get-tuple-element.15, f32[1024,2048]{1,0:T(8,128)S(1)} %copy-done.2, f32[]{:T(128)S(6)} %div.33), kind=kOutput, calls=%fused_computation.43 | convolution fusion | flops 12889096192 | bytes 12582916 | tf_op jit(solution)/shard_map/dot_general | solution.py:72
  272.4 2.7 fusion.16
  275.0 13.7 %fusion.23 = f32[1024,1024]{1,0:T(8,128)S(1)} fusion(f32[1024,1024]{1,0:T(8,128)S(1)} %get-tuple-element.16, f32[1024,2048]{1,0:T(8,128)S(1)} %copy-done.2, f32[]{:T(128)S(6)} %div.38), kind=kOutput, calls=%fused_computation.42 | convolution fusion | flops 12889096192 | bytes 12582916 | tf_op jit(solution)/shard_map/dot_general | solution.py:72
  288.7 2.5 fusion.15
  291.2 2.5 convolution_divide_fusion.1
  293.7 2.5 convolution_divide_fusion
  297.0 66.9 %all-gather.5.cloned.1.call-done = bf16[1024,2048]{1,0:T(8,128)(2,1)} async-done(((bf16[32,2048]{1,0:T(8,128)(2,1)}), bf16[1024,2048]{1,0:T(8,128)(2,1)}) %all-gather.5.cloned.1.call-update) | async-done | bytes 4194320 | tf_op jit(solution)/shard_map/all_gather | solution.py:84
  363.9 3.3 fusion.13
  367.2 2.5 fusion.11
  369.7 1.3 copy-done.3
  371.1 1.7 multiply_reduce_fusion
  372.7 75.5 %all-reduce = (f32[]{:T(128)}, f32[]{:T(128)}) all-reduce(f32[]{:T(128)} %get-tuple-element.17, f32[]{:T(128)} %multiply_reduce_fusion), channel_id=1, replica_groups=mesh['row'=32,'col'=8] {'row','col'}, use_global_device_ids=true, to_apply=%region_4.5 | all-reduce | flops 2 | bytes 16 | tf_op jit(solution)/shard_map/psum | solution.py:93
  449.5 3.4 multiply_convert_fusion
  (26 shorter events, 7.7 us)
Async XLA Ops:
  7.2 1.2 copy-start
  7.2 162.9 %reduce-scatter.4.cloned.1.call-start = ((), (), s32[]{:S(2)}) async-start(), calls=%async_computation.3 | async-start | bytes 8650752
  14.1 7.2 %collective-permute-start = (bf16[512,2048]{1,0:T(8,128)(2,1)S(1)}, bf16[512,2048]{1,0:T(8,128)(2,1)}, u32[]{:S(2)}, u32[]{:S(2)}) collective-permute-start(bf16[512,2048]{1,0:T(8,128)(2,1)S(1)} %get-tuple-element.18), channel_id=1, source_target_pairs={{0,8},{8,0},{16,24},{24,16},{32,40},{40,32},{48,56},{56,48},{64,72... | collective-permute-start | bytes 6291464 | tf_op jit(solution)/shard_map/ppermute | solution.py:18
  26.2 2.6 copy-start.6
  42.1 0.9 copy-start.4
  42.1 205.2 %all-gather.3.cloned.1.call-start = ((), (), s32[]{:S(2)}) async-start(), calls=%async_computation.1 | async-start | bytes 8650752 | tf_op jit(solution)/shard_map/all_gather | solution.py:52
  172.5 191.4 %all-gather.5.cloned.1.call-start = ((), (), s32[]{:S(2)}) async-start(), calls=%async_computation.2 | async-start | bytes 4325376 | tf_op jit(solution)/shard_map/all_gather | solution.py:84
  253.1 5.8 %copy-start.2 = (f32[1024,2048]{1,0:T(8,128)S(1)}, f32[1024,2048]{1,0:T(8,128)}, u32[]{:S(2)}) copy-start(f32[1024,2048]{1,0:T(8,128)} %all-gather.3.cloned.1.call-done) | copy-start | bytes 25165828
  363.9 3.3 copy-start.5
  369.7 1.3 copy-start.3
  371.1 81.9 %copy-start.1 = (bf16[1024,512]{1,0:T(8,128)(2,1)S(1)}, bf16[1024,512]{1,0:T(8,128)(2,1)}, u32[]{:S(2)}) copy-start(bf16[1024,512]{1,0:T(8,128)(2,1)} %param.5) | copy-start | bytes 3145732
Sparse Core Ops, SparseCore 0:
  42.3 127.7 reduce-scatter.3
  172.6 74.6 all-gather.2
  297.1 66.6 all-gather.4
where the time goes:
time: 468 us; the launch traced here: 460 us
  waiting for transfers between devices  272 us (58%)
  blocking collectives  75.5 us (16%)
  matrix products  56.4 us (12%)
  other arithmetic  19.5 us (4%)
  between operations  16.9 us (4%)
  local copies, waits for them, and re-layouts  15.9 us (3%)
    unnamed x4, waiting for transfers between devices  127 us
    psum x1, blocking collectives, shards(): lax.psum((grad_square, prod_square), ('row', 'col'))  75.5 us
    all_gather x1, waiting for transfers between devices, shards(): full_stats = lax.all_gather(new_stats, 'row', axis=0, tiled=True)  74.8 us
    all_gather x1, waiting for transfers between devices, shards(): piece = lax.all_gather(roots_half, 'row', axis=0, tiled=True)  66.9 us
    dot_general x2, matrix products, shards(): jnp.dot(starts[k], factors[k], precision=lax.Precision.HIGHEST)  27.2 us
    unnamed x17, local copies, waits for them, and re-layouts  14.9 us
  transfers between devices with their start and end apart: 4, of which 4 were waited for; matrix products, arithmetic and copies ran while one was open for 0% of the time, Pallas kernels for 0%

commit v1 on v0

--- a/solution.py
+++ b/solution.py
@@ -81,7 +81,8 @@
     new_roots = jnp.concatenate(root_pieces, 1)
     roots_half = new_roots.astype(jnp.bfloat16)
     empty = jnp.zeros((weight_rows, weight_cols), jnp.float32)
-    piece = lax.all_gather(roots_half, "row", axis=0, tiled=True)
+    sent = jnp.stack([roots_half] * lax.axis_size("row"))
+    piece = jnp.concatenate(lax.all_to_all(sent, "row", 0, 0), axis=0)
     terms = []
     for index_block in range(block_count):
         left = lax.dynamic_slice_in_dim(whitened, index_block * block_size, piece.shape[0], 1)

time: 468 us -> 500 us (1.068)
  blocking collectives: 75.5 us -> 178 us
  waiting for transfers between devices: 272 us -> 205 us
    all_to_all x0 -> x1, blocking collectives: none -> 102 us  [shards(): piece = jnp.concatenate(lax.all_to_all(sent, 'row', 0, 0), axis=0)]
    all_gather x1 -> x0, waiting for transfers between devices: 66.9 us -> none  [shards(): piece = lax.all_gather(roots_half, 'row', axis=0, tiled=True)]
    unnamed x4 -> x3, waiting for transfers between devices: 127 us -> 127 us
  transfers between devices with their start and end apart: 4 -> 3, of which waited for: 4 -> 3; matrix products, arithmetic and copies ran while one was open for 0% -> 0% of each run, Pallas kernels for 0% -> 0%
where the time goes in v1:
time: 500 us; the launch traced here: 492 us
  waiting for transfers between devices  205 us (41%)
  blocking collectives  178 us (36%)
  matrix products  53.1 us (11%)
  other arithmetic  19.4 us (4%)
  between operations  17.1 us (3%)
  local copies, waits for them, and re-layouts  16.4 us (3%)
    unnamed x3, waiting for transfers between devices  127 us
    all_to_all x1, blocking collectives, shards(): piece = jnp.concatenate(lax.all_to_all(sent, 'row', 0, 0), axis=0)  102 us
    psum x1, blocking collectives, shards(): lax.psum((grad_square, prod_square), ('row', 'col'))  75.9 us
    all_gather x1, waiting for transfers between devices, shards(): full_stats = lax.all_gather(new_stats, 'row', axis=0, tiled=True)  74.6 us
    dot_general x2, matrix products, shards(): jnp.dot(starts[k], factors[k], precision=lax.Precision.HIGHEST)  27.2 us
    unnamed x17, local copies, waits for them, and re-layouts  14.9 us
  transfers between devices with their start and end apart: 3, of which 3 were waited for; matrix products, arithmetic and copies ran while one was open for 0% of the time, Pallas kernels for 0%

profile of v1, /device:TPU:1, one launch (start us, length us, event | category | flops | bytes accessed | tf_op | source)
XLA Modules:
  0.0 492.2 jit_solution(3377409923242977265)
XLA Ops:
  8.4 5.7 %multiply_reduce_fusion.1 = (f32[]{:T(128)}, bf16[512,2048]{1,0:T(8,128)(2,1)S(1)}) fusion(bf16[1024,512]{1,0:T(8,128)(2,1)S(1)} %copy-done, bf16[1024,2048]{1,0:T(8,128)(2,1)} %param.4), kind=kOutput, calls=%fused_computation.15 | convolution fusion | flops 2151677952 | bytes 7340036 | tf_op jit(solution)/shard_map/dot_general | solution.py:29
  14.1 3.2 collective-permute-start
  17.4 3.9 collective-permute-done
  21.3 4.9 fusion.10
  26.2 1.3 fusion.18
  27.5 1.3 fusion.21
  28.8 4.1 pad_maximum_fusion
  32.9 9.2 %copy.12 = f32[1024,2048]{1,0:T(8,128)} copy(f32[1024,2048]{0,1:T(8,128)} %pad_maximum_fusion) | data formatting | bytes 16777216
  43.3 126.8 %reduce-scatter.4.cloned.1.call-done = f32[32,2048]{1,0:T(8,128)} async-done(((f32[1024,2048]{1,0:T(8,128)}), f32[32,2048]{1,0:T(8,128)}) %reduce-scatter.4.cloned.1.call-update) | async-done | bytes 262160
  170.1 1.3 copy.13
  172.6 74.6 %all-gather.2.cloned.1.call-done = f32[1024,2048]{1,0:T(8,128)} async-done(((f32[32,2048]{1,0:T(8,128)}), f32[1024,2048]{1,0:T(8,128)}) %all-gather.2.cloned.1.call-update) | async-done | bytes 8388624 | tf_op jit(solution)/shard_map/all_gather | solution.py:52
  247.2 4.2 select_reduce_fusion.1
  252.7 5.1 %select_subtract_fusion.1 = (f32[1024,1024]{1,0:T(8,128)S(1)}, f32[1024,1024]{1,0:T(8,128)S(1)}) fusion(f32[]{:T(128)S(6)} %div.33, f32[1024,2048]{1,0:T(8,128)} %all-gather.2.cloned.1.call-done, f32[]{:T(128)S(6)} %div.38), kind=kLoop, calls=%fused_computation.4 | loop fusion | flops 11534336 | bytes 16777224 | tf_op jit(solution)/shard_map/sub | solution.py:70
  258.6 13.5 %fusion.25 = f32[1024,1024]{1,0:T(8,128)S(1)} fusion(f32[1024,1024]{1,0:T(8,128)S(1)} %get-tuple-element.15, f32[1024,2048]{1,0:T(8,128)S(1)} %copy-done.2, f32[]{:T(128)S(6)} %div.33), kind=kOutput, calls=%fused_computation.43 | convolution fusion | flops 12889096192 | bytes 12582916 | tf_op jit(solution)/shard_map/dot_general | solution.py:72
  272.0 2.7 fusion.16
  274.7 13.7 %fusion.23 = f32[1024,1024]{1,0:T(8,128)S(1)} fusion(f32[1024,1024]{1,0:T(8,128)S(1)} %get-tuple-element.16, f32[1024,2048]{1,0:T(8,128)S(1)} %copy-done.2, f32[]{:T(128)S(6)} %div.38), kind=kOutput, calls=%fused_computation.42 | convolution fusion | flops 12889096192 | bytes 12582916 | tf_op jit(solution)/shard_map/dot_general | solution.py:72
  288.4 2.5 fusion.15
  290.9 2.5 convolution_divide_fusion.1
  293.4 2.5 convolution_divide_fusion
  297.2 101.8 %all_to_all.5 = bf16[32,32,2048]{2,1,0:T(8,128)(2,1)S(1)} all-to-all(bf16[32,32,2048]{2,1,0:T(8,128)(2,1)S(1)} %stack.2), channel_id=1, replica_groups=mesh['row'=32,'col'=8] {'row'}, dimensions={0} | all-to-all | bytes 8388608 | tf_op jit(solution)/shard_map/all_to_all | solution.py:85
  401.5 1.3 copy-done.3
  402.8 1.7 multiply_reduce_fusion
  404.5 75.9 %all-reduce = (f32[]{:T(128)}, f32[]{:T(128)}) all-reduce(f32[]{:T(128)} %get-tuple-element.17, f32[]{:T(128)} %multiply_reduce_fusion), channel_id=1, replica_groups=mesh['row'=32,'col'=8] {'row','col'}, use_global_device_ids=true, to_apply=%region_4.5 | all-reduce | flops 2 | bytes 16 | tf_op jit(solution)/shard_map/psum | solution.py:94
  481.7 3.4 multiply_convert_fusion
  (25 shorter events, 8.1 us)
Async XLA Ops:
  7.2 1.2 copy-start
  7.2 162.9 %reduce-scatter.4.cloned.1.call-start = ((), (), s32[]{:S(2)}) async-start(), calls=%async_computation.3 | async-start | bytes 8650752
  14.1 7.2 %collective-permute-start = (bf16[512,2048]{1,0:T(8,128)(2,1)S(1)}, bf16[512,2048]{1,0:T(8,128)(2,1)}, u32[]{:S(2)}, u32[]{:S(2)}) collective-permute-start(bf16[512,2048]{1,0:T(8,128)(2,1)S(1)} %get-tuple-element.18), channel_id=1, source_target_pairs={{0,8},{8,0},{16,24},{24,16},{32,40},{40,32},{48,56},{56,48},{64,72... | collective-permute-start | bytes 6291464 | tf_op jit(solution)/shard_map/ppermute | solution.py:18
  26.2 2.6 copy-start.5
  42.0 0.9 copy-start.4
  42.1 205.1 %all-gather.2.cloned.1.call-start = ((), (), s32[]{:S(2)}) async-start(), calls=%async_computation.2 | async-start | bytes 8650752 | tf_op jit(solution)/shard_map/all_gather | solution.py:52
  252.7 5.8 %copy-start.2 = (f32[1024,2048]{1,0:T(8,128)S(1)}, f32[1024,2048]{1,0:T(8,128)}, u32[]{:S(2)}) copy-start(f32[1024,2048]{1,0:T(8,128)} %all-gather.2.cloned.1.call-done) | copy-start | bytes 25165828
  297.2 101.8 %copy-start.6 = (bf16[512,2048]{0,1:T(8,128)(2,1)S(1)}, bf16[512,2048]{0,1:T(8,128)(2,1)}, u32[]{:S(2)}) copy-start(bf16[512,2048]{0,1:T(8,128)(2,1)} %copy-done.5) | copy-start | bytes 6291460
  401.5 1.3 copy-start.3
  402.8 82.3 %copy-start.1 = (bf16[1024,512]{1,0:T(8,128)(2,1)S(1)}, bf16[1024,512]{1,0:T(8,128)(2,1)}, u32[]{:S(2)}) copy-start(bf16[1024,512]{1,0:T(8,128)(2,1)} %param.5) | copy-start | bytes 3145732
Sparse Core Ops, SparseCore 0:
  42.2 127.8 reduce-scatter.3
  172.7 74.4 all-gather.1
